TPU v7x, 32 devices: a whole 2x2x4 slice. The times are simulated.
32 devices in a mesh: freq: 2 (over core), vs: 16 (over z, y, x).
Axes of the slice: x: 2, y: 2, z: 4, core: 2. Of those that a mesh axis runs over, the one named last changes fastest.
Arguments:
- kernel: bfloat16 [4, 2, 256, 16384], P('freq', None, None, 'vs'), may hold values from -0.03125 to 0.03125
- sources: bfloat16 [4, 2, 512, 16384], P('freq', None, 'vs'), may hold values from -6 to 6
- observed: float32 [256, 160, 512], P('freq', None, 'vs'), may hold values from -6 to 6
- gate_start: int32 [256], P('freq'), may hold values from 0 to 80, as said below
- gate_length: int32 [256], P('freq'), may hold values from 1 to 160
Outputs:
- gradient: bfloat16 [4, 2, 512, 16384], P('freq', None, 'vs')
- misfit: float32 [256, 160, 512], P('freq', None, 'vs')
Inputs may be any that keep to these rules, and one draw needn't show every extreme that they name: gate_start + gate_length <= 160 for every receiver.
All inputs are finite; a program needn't handle non-finite values.
Results may differ from a plain program's by a relative error of at most 0.0057.
Values may be sent and summed in bfloat16 or wider, within the bound.
A program may use at most 128 MiB of HBM per device.

v0:
```python
import jax
import jax.numpy as jnp
from jax import lax
from jax.sharding import PartitionSpec as P

NS = 16384
RW = 256


def complex_apply(kern, model):
    form = "frs,fvs->frv"
    real_part = jnp.einsum(
        form, kern[:, 0], model[:, 0], preferred_element_type=jnp.float32
    ) - jnp.einsum(form, kern[:, 1], model[:, 1], preferred_element_type=jnp.float32)
    imag_part = jnp.einsum(
        form, kern[:, 0], model[:, 1], preferred_element_type=jnp.float32
    ) + jnp.einsum(form, kern[:, 1], model[:, 0], preferred_element_type=jnp.float32)
    return jnp.stack([real_part, imag_part], 1)


def complex_adjoint(kern, spectrum):
    form = "frv,frs->fvs"
    real_part = jnp.einsum(
        form, spectrum[:, 0], kern[:, 0], preferred_element_type=jnp.float32
    ) + jnp.einsum(form, spectrum[:, 1], kern[:, 1], preferred_element_type=jnp.float32)
    imag_part = jnp.einsum(
        form, spectrum[:, 1], kern[:, 0], preferred_element_type=jnp.float32
    ) - jnp.einsum(form, spectrum[:, 0], kern[:, 1], preferred_element_type=jnp.float32)
    factor = (NS / RW) ** 0.5
    return factor * jnp.stack([real_part, imag_part], 1)


def transform_tables(count, samples):
    sample_index = jnp.arange(samples, dtype=jnp.int32)
    bin_index = samples // 4 + jnp.arange(count, dtype=jnp.int32)
    phase = sample_index[:, None] * bin_index[None, :] % samples
    theta = 2.0 * jnp.pi / samples * phase.astype(jnp.float32)
    return (jnp.cos(theta), jnp.sin(theta))


def local(kernel, sources, observed, gate_start, gate_length):
    gathered = lax.all_gather(kernel, "vs", axis=3, tiled=True)
    forward = complex_apply(gathered, sources)
    field = forward.astype(jnp.bfloat16)
    timed = lax.all_to_all(field, "freq", split_axis=2, concat_axis=0, tiled=True)
    count = timed.shape[0]
    samples = observed.shape[1]
    cosine, sine = transform_tables(count, samples)
    scale = count ** (-0.5)
    values = timed.astype(jnp.float32)
    highest = lax.Precision.HIGHEST
    signal = scale * (
        jnp.einsum("tf,frv->rtv", cosine, values[:, 0], precision=highest)
        - jnp.einsum("tf,frv->rtv", sine, values[:, 1], precision=highest)
    )
    sample_index = jnp.arange(samples, dtype=jnp.int32)
    inside = (sample_index[None, :] >= gate_start[:, None]) & (
        sample_index[None, :] < (gate_start + gate_length)[:, None]
    )
    gate_mask = inside.astype(jnp.float32)
    misfit = gate_mask[:, :, None] * (signal - observed)
    back_real = scale * jnp.einsum("tf,rtv->frv", cosine, misfit, precision=highest)
    back_imag = -scale * jnp.einsum("tf,rtv->frv", sine, misfit, precision=highest)
    back_spectrum = jnp.stack([back_real, back_imag], 1).astype(jnp.bfloat16)
    spectral = lax.all_to_all(back_spectrum, "freq", split_axis=0, concat_axis=2, tiled=True)
    gradient = complex_adjoint(gathered, spectral).astype(jnp.bfloat16)
    return (gradient, misfit)


def solution(mesh):
    return jax.shard_map(
        local,
        mesh=mesh,
        in_specs=(
            P("freq", None, None, "vs"),
            P("freq", None, "vs", None),
            P("freq", None, "vs"),
            P("freq"),
            P("freq"),
        ),
        out_specs=(P("freq", None, "vs", None), P("freq", None, "vs")),
        check_vma=False,
    )
```

profile of v0, /device:TPU:0, one launch (start us, length us, event | category | flops | bytes accessed | tf_op | source)
XLA Modules:
  0.0 469.7 jit_solution(584789659797652340)
XLA Ops:
  7.2 0.0 copy-start.1
  7.2 0.0 copy-start.3
  7.2 0.0 all-gather.2.cloned.1.call-start
  7.2 3.1 copy.15
  10.3 0.0 all-gather.2.cloned.1.call-update
  10.3 0.0 copy-done.1
  10.3 0.0 copy-done.3
  10.4 365.5 %all-gather.2.cloned.1.call-done = bf16[2,2,256,16384]{3,2,0,1:T(8,128)(2,1)} async-done(((bf16[2,2,256,1024]{3,2,0,1:T(8,128)(2,1)}), bf16[2,2,256,16384]{3,2,0,1:T(8,128)(2,1)}) %all-gather.2.cloned.1.call-update) | async-done | bytes 33554448 | tf_op jit(solution)/shard_map/all_gather | solution.py:42
  375.9 0.0 copy-start.2
  375.9 10.0 %fusion.4 = f32[2,256,32]{1,2,0:T(8,128)S(1)} fusion(bf16[2,2,256,16384]{3,2,0,1:T(8,128)(2,1)} %all-gather.2.cloned.1.call-done, bf16[2,2,32,16384]{3,2,1,0:T(8,128)(2,1)} %param.6), kind=kOutput, calls=%fused_computation.8 | convolution fusion | flops 536870912 | bytes 18939904 | tf_op jit(solution)/shard_map/frs,fvs->frv/dot_general | solution.py:15
  385.8 0.0 copy-done.2
  385.9 8.6 %fusion.5 = f32[2,256,32]{1,2,0:T(8,128)S(1)} fusion(bf16[2,2,256,16384]{3,2,0,1:T(8,128)(2,1)} %all-gather.2.cloned.1.call-done, bf16[2,2,32,16384]{3,2,1,0:T(8,128)(2,1)S(1)} %copy-done.2), kind=kOutput, calls=%fused_computation.9 | convolution fusion | flops 536870912 | bytes 18939904 | tf_op jit(solution)/shard_map/frs,fvs->frv/dot_general | solution.py:12
  394.5 8.6 %fusion.37 = bf16[2,1,256,32]{2,3,0,1:T(8,128)(2,1)S(1)} fusion(f32[2,256,32]{1,2,0:T(8,128)S(1)} %fusion.4, bf16[2,2,32,16384]{3,2,1,0:T(8,128)(2,1)S(1)} %copy-done.2, bf16[2,2,256,16384]{3,2,0,1:T(8,128)(2,1)} %all-gather.2.cloned.1.call-done), kind=kOutput, calls=%fused_computation.35 | convolution fusion | flops 536903680 | bytes 18972672 | tf_op jit(solution)/shard_map/frs,fvs->frv/dot_general | solution.py:17
  403.1 8.6 %fusion.34 = bf16[2,1,256,32]{2,3,0,1:T(8,128)(2,1)S(1)} fusion(f32[2,256,32]{1,2,0:T(8,128)S(1)} %fusion.5, bf16[2,2,32,16384]{3,2,1,0:T(8,128)(2,1)S(1)} %copy-done.2, bf16[2,2,256,16384]{3,2,0,1:T(8,128)(2,1)} %all-gather.2.cloned.1.call-done), kind=kOutput, calls=%fused_computation.34 | convolution fusion | flops 536903680 | bytes 18972672 | tf_op jit(solution)/shard_map/frs,fvs->frv/dot_general | solution.py:14
  411.8 0.0 copy-start
  411.8 0.2 copy.18
  412.0 0.3 reshape.54
  412.3 3.9 all_to_all.36
  416.2 0.2 reshape.55
  416.4 0.1 copy.19
  416.5 1.3 fusion.42
  417.9 0.0 copy-done
  417.9 3.0 fusion.9
  420.9 1.4 fusion.32
  422.3 1.4 fusion.33
  423.7 3.0 copy.24
  426.8 3.8 all_to_all.37
  430.6 0.1 copy.29
  430.7 7.3 %fusion.2 = f32[2,32,16384]{2,1,0:T(8,128)S(1)} fusion(bf16[2,2,256,16384]{3,2,0,1:T(8,128)(2,1)} %all-gather.2.cloned.1.call-done, bf16[2,2,256,32]{2,3,0,1:T(8,128)(2,1)S(1)} %all_to_all.33), kind=kOutput, calls=%fused_computation.6 | convolution fusion | flops 536870912 | bytes 21004288 | tf_op jit(solution)/shard_map/frv,frs->fvs/dot_general | solution.py:26
  438.0 7.3 %fusion.3 = f32[2,32,16384]{2,1,0:T(8,128)S(1)} fusion(bf16[2,2,256,16384]{3,2,0,1:T(8,128)(2,1)} %all-gather.2.cloned.1.call-done, bf16[2,2,256,32]{2,3,0,1:T(8,128)(2,1)S(1)} %all_to_all.33), kind=kOutput, calls=%fused_computation.7 | convolution fusion | flops 536870912 | bytes 21004288 | tf_op jit(solution)/shard_map/frv,frs->fvs/dot_general | solution.py:23
  445.4 7.3 %fusion.1 = f32[2,1,32,16384]{3,2,0,1:T(8,128)S(1)} fusion(f32[2,32,16384]{2,1,0:T(8,128)S(1)} %fusion.2, bf16[2,2,256,16384]{3,2,0,1:T(8,128)(2,1)} %all-gather.2.cloned.1.call-done, bf16[2,2,256,32]{2,3,0,1:T(8,128)(2,1)S(1)} %all_to_all.33), kind=kOutput, calls=%fused_computation.3 | convolution fusion | flops 537919488 | bytes 25198592 | tf_op jit(solution)/shard_map/frv,frs->fvs/dot_general | solution.py:28
  452.7 7.3 %fusion = f32[2,1,32,16384]{3,2,0,1:T(8,128)S(1)} fusion(f32[2,32,16384]{2,1,0:T(8,128)S(1)} %fusion.3, bf16[2,2,256,16384]{3,2,0,1:T(8,128)(2,1)} %all-gather.2.cloned.1.call-done, bf16[2,2,256,32]{2,3,0,1:T(8,128)(2,1)S(1)} %all_to_all.33), kind=kOutput, calls=%fused_computation.2 | convolution fusion | flops 537919488 | bytes 25198592 | tf_op jit(solution)/shard_map/frv,frs->fvs/dot_general | solution.py:25
  460.0 0.5 fusion.8
  460.5 2.3 copy.23
  (7 shorter events, 0.1 us)
Async XLA Ops:
  7.2 3.2 copy-start.1
  7.2 3.2 copy-start.3
  7.2 368.7 %all-gather.2.cloned.1.call-start = ((), (), s32[]{:S(2)}) async-start(), calls=%async_computation.2 | async-start | bytes 35651584 | tf_op jit(solution)/shard_map/all_gather | solution.py:42
  375.9 10.0 %copy-start.2 = (bf16[2,2,32,16384]{3,2,1,0:T(8,128)(2,1)S(1)}, bf16[2,2,32,16384]{3,2,1,0:T(8,128)(2,1)}, u32[]{:S(2)}) copy-start(bf16[2,2,32,16384]{3,2,1,0:T(8,128)(2,1)} %param.6) | copy-start | bytes 12582916
  411.8 6.1 %copy-start = (f32[128,160,32]{0,2,1:T(8,128)S(1)}, f32[128,160,32]{0,2,1:T(8,128)}, u32[]{:S(2)}) copy-start(f32[128,160,32]{0,2,1:T(8,128)} %param.7) | copy-start | bytes 7864324
Sparse Core Ops, SparseCore 0:
  11.3 364.5 all-gather.1
where the time goes:
time: 470 us
  waiting for transfers between devices  365 us (78%)
  matrix products  72.3 us (15%)
  between operations  14.2 us (3%)
  local copies, waits for them, and re-layouts  9.35 us (2%)
  blocking collectives  7.71 us (2%)
    all_gather x1, waiting for transfers between devices, local(): gathered = lax.all_gather(kernel, 'vs', axis=3, tiled=True)  365 us
    dot_general x1, matrix products, complex_apply(): jnp.einsum(form, kern[:, 0], model[:, 1], preferred_element_type=jnp.floa...  9.96 us
  transfers between devices with their start and end apart: 1, of which 1 were waited for; matrix products, arithmetic and copies ran while one was open for 0% of the time, Pallas kernels for 0%

commit v1 on v0

v1 whole, which is shorter than its diff:
```python
import functools

import numpy as np

import jax
import jax.numpy as jnp
from jax import lax
from jax.experimental import pallas as pl
from jax.experimental.pallas import tpu as pltpu
from jax.sharding import PartitionSpec as P

MESH = pl.DeviceIdType.MESH


def transform_tables(count, samples):
    sample_index = np.arange(samples)
    bin_index = samples // 4 + np.arange(count)
    phase = sample_index[None, :] * bin_index[:, None] % samples
    theta = 2.0 * np.pi / samples * phase
    scale = count ** (-0.5)
    return np.stack([scale * np.cos(theta), -scale * np.sin(theta)], 1).astype(np.float32)


def body(n, nf, factor, k_hbm, x_hbm, obs_hbm, table, gate, grad_hbm, mis_hbm,
         kbuf, xbuf, pbuf, rbuf, fbuf, obuf, bsend, brecv, gbuf,
         lsem, xs, xr, ps, pr, bs, br, gs, gr):
    f = lax.axis_index("freq")
    me = lax.axis_index("vs")
    local_f, rw = kbuf.shape[0], kbuf.shape[2]
    span = kbuf.shape[3]
    samples, nv, half = obuf.shape

    k_copy = pltpu.make_async_copy(k_hbm, kbuf, lsem.at[0])
    o_copy = pltpu.make_async_copy(obs_hbm, obuf, lsem.at[1])
    m_copy = pltpu.make_async_copy(obuf, mis_hbm, lsem.at[2])

    def columns(j):
        return pl.ds(pl.multiple_of(j * span, span), span)

    def peer(d):
        return lax.rem(me + d, n)

    def origin(d):
        return lax.rem(me + n - d, n)

    def other(e):
        return lax.rem(f + e, nf)

    def x_send(j):
        return pltpu.make_async_remote_copy(
            x_hbm.at[:, :, :, columns(j)], xbuf.at[me], xs.at[j], xr.at[me],
            device_id=(f, j), device_id_type=MESH)

    def x_recv(j):
        return pltpu.make_async_remote_copy(
            x_hbm.at[:, :, :, columns(j)], xbuf.at[j], xs.at[j], xr.at[j],
            device_id=(f, j), device_id_type=MESH)

    def p_send(j, h):
        return pltpu.make_async_remote_copy(
            pbuf.at[j, h], rbuf.at[me, f], ps.at[j, h], pr.at[me, f],
            device_id=(h, j), device_id_type=MESH)

    def p_recv(j, h):
        return pltpu.make_async_remote_copy(
            pbuf.at[j, h], rbuf.at[j, h], ps.at[j, h], pr.at[j, h],
            device_id=(h, j), device_id_type=MESH)

    def b_send(j, h):
        return pltpu.make_async_remote_copy(
            bsend.at[h], brecv.at[me, f], bs.at[j, h], br.at[me, f],
            device_id=(h, j), device_id_type=MESH)

    def b_recv(j, h):
        return pltpu.make_async_remote_copy(
            bsend.at[h], brecv.at[j, h], bs.at[j, h], br.at[j, h],
            device_id=(h, j), device_id_type=MESH)

    def g_send(j):
        return pltpu.make_async_remote_copy(
            gbuf.at[j], grad_hbm.at[:, :, :, columns(me)], gs.at[j], gr.at[me],
            device_id=(f, j), device_id_type=MESH)

    def g_recv(j):
        return pltpu.make_async_remote_copy(
            gbuf.at[j], grad_hbm.at[:, :, :, columns(j)], gs.at[j], gr.at[j],
            device_id=(f, j), device_id_type=MESH)

    x_own = pltpu.make_async_copy(x_hbm.at[:, :, :, columns(me)], xbuf.at[me], xr.at[me])
    p_own = pltpu.make_async_copy(pbuf.at[me, f], rbuf.at[me, f], pr.at[me, f])
    b_own = pltpu.make_async_copy(bsend.at[f], brecv.at[me, f], br.at[me, f])
    g_own = pltpu.make_async_copy(gbuf.at[me], grad_hbm.at[:, :, :, columns(me)], gr.at[me])

    barrier = pltpu.get_barrier_semaphore()
    for e in range(1, nf):
        pl.semaphore_signal(barrier, inc=1, device_id=(other(e), me), device_id_type=MESH)

    @pl.loop(1, n)
    def _(d):
        for e in range(nf):
            pl.semaphore_signal(barrier, inc=1, device_id=(other(e), peer(d)), device_id_type=MESH)

    k_copy.start()
    x_own.start()
    o_copy.start()
    pl.semaphore_wait(barrier, n * nf - 1)

    @pl.loop(1, n)
    def _(d):
        x_send(peer(d)).start()

    k_copy.wait()

    def forward(j):
        for i in range(local_f):
            xr_, xi_ = xbuf[j, i, 0], xbuf[j, i, 1]
            kr_, ki_ = kbuf[i, 0], kbuf[i, 1]
            x2 = jnp.concatenate([xr_, xi_], 0)
            dims = (((1,), (1,)), ((), ()))
            pr_ = lax.dot_general(x2, kr_, dims, preferred_element_type=jnp.float32)
            pi_ = lax.dot_general(x2, ki_, dims, preferred_element_type=jnp.float32)
            real = (pr_[:nv] - pi_[nv:]).astype(jnp.bfloat16)
            imag = (pr_[nv:] + pi_[:nv]).astype(jnp.bfloat16)
            for h in range(nf):
                pbuf[j, h, i, 0] = real[:, h * half:(h + 1) * half]
                pbuf[j, h, i, 1] = imag[:, h * half:(h + 1) * half]

    x_own.wait()
    forward(me)
    p_own.start()
    for e in range(1, nf):
        p_send(me, other(e)).start()

    @pl.loop(1, n)
    def _(d):
        j = origin(d)
        x_recv(j).wait_recv()
        forward(j)
        for e in range(nf):
            p_send(j, other(e)).start()

    p_own.wait()
    for e in range(1, nf):
        p_recv(me, other(e)).wait_recv()

    @pl.loop(1, n)
    def _(d):
        for e in range(nf):
            p_recv(origin(d), other(e)).wait_recv()

    for h in range(nf):
        for i in range(local_f):
            for c in range(2):
                def add(q, total):
                    return total + rbuf[q, h, i, c].astype(jnp.float32)
                total = lax.fori_loop(0, n, add, jnp.zeros((nv, half), jnp.float32))
                fbuf[h * local_f + i, c] = total.astype(jnp.bfloat16).astype(jnp.float32)

    o_copy.wait()
    count = nf * local_f
    opens = gate[0:1, :]
    closes = gate[1:2, :]
    rows = 16
    for part in range(nv // rows):
        sl = slice(part * rows, (part + 1) * rows)
        fields = [fbuf[q, c, sl] for q in range(count) for c in range(2)]

        def sample(t, totals):
            weights = [table[q * samples + t] for q in range(2 * count)]
            signal = fields[0] * weights[0]
            for q in range(1, 2 * count):
                signal = signal + fields[q] * weights[q]
            inside = (opens <= t) & (t < closes)
            misfit = jnp.where(inside, signal - obuf[t, sl], 0.0)
            obuf[t, sl] = misfit
            return tuple(totals[q] + misfit * weights[q] for q in range(2 * count))

        zero = jnp.zeros((rows, half), jnp.float32)
        totals = lax.fori_loop(0, samples, sample, (zero,) * (2 * count))
        for q in range(count):
            for c in range(2):
                bsend[q // local_f, q % local_f, c, sl] = totals[2 * q + c].astype(jnp.bfloat16)

    b_own.start()
    for e in range(1, nf):
        b_send(me, other(e)).start()

    @pl.loop(1, n)
    def _(d):
        for e in range(nf):
            b_send(peer(d), other(e)).start()

    m_copy.start()

    def backward(j):
        for i in range(local_f):
            b_r = jnp.concatenate([brecv[j, h, i, 0] for h in range(nf)], 1)
            b_i = jnp.concatenate([brecv[j, h, i, 1] for h in range(nf)], 1)
            left = jnp.concatenate([b_r, b_i], 0)
            right = jnp.concatenate([b_i, -b_r], 0)
            out = jnp.dot(left, kbuf[i, 0], preferred_element_type=jnp.float32)
            out = out + jnp.dot(right, kbuf[i, 1], preferred_element_type=jnp.float32)
            out = (factor * out).astype(jnp.bfloat16)
            gbuf[j, i, 0] = out[:nv]
            gbuf[j, i, 1] = out[nv:]

    b_own.wait()
    for e in range(1, nf):
        b_recv(me, other(e)).wait_recv()
    backward(me)
    g_own.start()

    @pl.loop(1, n)
    def _(d):
        j = origin(d)
        for e in range(nf):
            b_recv(j, other(e)).wait_recv()
        backward(j)
        g_send(j).start()

    for e in range(1, nf):
        p_send(me, other(e)).wait_send()
        b_send(me, other(e)).wait_send()

    @pl.loop(1, n)
    def _(d):
        j = origin(d)
        x_send(j).wait_send()
        for e in range(nf):
            p_send(j, other(e)).wait_send()
            b_send(j, other(e)).wait_send()
        g_send(j).wait_send()
        g_recv(j).wait_recv()

    g_own.wait()
    m_copy.wait()


def local(n, nf, kernel, sources, observed, gate_start, gate_length):
    local_f, _, rw, span = kernel.shape
    nv, ns = sources.shape[2:]
    half, samples = observed.shape[:2]
    count = nf * local_f
    table = jnp.asarray(transform_tables(count, samples).reshape(-1))
    gate = jnp.stack([gate_start, gate_start + gate_length])
    piece = (local_f, 2, nv, half)
    any_spec = pl.BlockSpec(memory_space=pl.ANY)
    dma = pltpu.SemaphoreType.DMA
    gradient, misfit = pl.pallas_call(
        functools.partial(body, n, nf, (ns / rw) ** 0.5),
        out_shape=(
            jax.ShapeDtypeStruct(sources.shape, jnp.bfloat16),
            jax.ShapeDtypeStruct((samples, nv, half), jnp.float32),
        ),
        in_specs=[any_spec, any_spec, any_spec,
                  pl.BlockSpec(memory_space=pltpu.SMEM),
                  pl.BlockSpec(memory_space=pltpu.VMEM)],
        out_specs=(any_spec, any_spec),
        scratch_shapes=[
            pltpu.VMEM(kernel.shape, jnp.bfloat16),
            pltpu.VMEM((n, local_f, 2, nv, span), jnp.bfloat16),
            pltpu.VMEM((n, nf) + piece, jnp.bfloat16),
            pltpu.VMEM((n, nf) + piece, jnp.bfloat16),
            pltpu.VMEM((count, 2, nv, half), jnp.float32),
            pltpu.VMEM((samples, nv, half), jnp.float32),
            pltpu.VMEM((nf,) + piece, jnp.bfloat16),
            pltpu.VMEM((n, nf) + piece, jnp.bfloat16),
            pltpu.VMEM((n, local_f, 2, nv, span), jnp.bfloat16),
            dma((3,)), dma((n,)), dma((n,)),
            dma((n, nf)), dma((n, nf)), dma((n, nf)), dma((n, nf)),
            dma((n,)), dma((n,)),
        ],
        compiler_params=pltpu.CompilerParams(
            collective_id=0, has_side_effects=True, vmem_limit_bytes=40 << 20),
    )(kernel, sources, observed.transpose(1, 2, 0), table, gate)
    return gradient, misfit.transpose(2, 0, 1)


def solution(mesh):
    n, nf = mesh.shape["vs"], mesh.shape["freq"]
    return jax.shard_map(
        functools.partial(local, n, nf),
        mesh=mesh,
        in_specs=(
            P("freq", None, None, "vs"),
            P("freq", None, "vs", None),
            P("freq", None, "vs"),
            P("freq"),
            P("freq"),
        ),
        out_specs=(P("freq", None, "vs", None), P("freq", None, "vs")),
        check_vma=False,
    )
```

time: 470 us -> 279 us (0.59)
  waiting for transfers between devices: 365 us -> 0 us
  Pallas kernels: 0 us -> 269 us
  matrix products: 72.3 us -> 0 us
  between operations: 14.2 us -> 0.64 us
  blocking collectives: 7.71 us -> 0 us
    all_gather x1 -> x0, waiting for transfers between devices: 365 us -> none  [local(): gathered = lax.all_gather(kernel, 'vs', axis=3, tiled=True)]
    pallas_call x0 -> x1, Pallas kernels: none -> 269 us  [local(): pl.pallas_call(functools.partial(body, n, nf, (ns / rw) ** 0.5), out_shap...]
    dot_general x12 -> x0, matrix products: 72.3 us -> none  [the longest x1 9.96 us: complex_apply(): jnp.einsum(form, kern[:, 0], model[:, 1], preferred_element_type=jnp.floa...]
    all_to_all x2 -> x0, blocking collectives: 7.71 us -> none  [the longest x1 3.92 us: local(): lax.all_to_all(field, 'freq', split_axis=2, concat_axis=0, tiled=True)]
  transfers between devices with their start and end apart: 1 -> 0, of which waited for: 1 -> 0; matrix products, arithmetic and copies ran while one was open for 0% -> 0% of each run, Pallas kernels for 0% -> 0%
where the time goes in v1:
time: 279 us
  Pallas kernels  269 us (96%)
  local copies, waits for them, and re-layouts  7.53 us (3%)
    pallas_call x1, Pallas kernels, local(): pl.pallas_call(functools.partial(body, n, nf, (ns / rw) ** 0.5), out_shap...  269 us
    unnamed x8, local copies, waits for them, and re-layouts  7.53 us

profile of v1, /device:TPU:0, one launch (start us, length us, event | category | flops | bytes accessed | tf_op | source)
XLA Modules:
  0.0 278.9 jit_solution(7230075602794182918)
XLA Ops:
  0.6 0.7 add_bitcast_fusion
  1.3 0.7 pad_add_fusion.gate
  2.0 0.0 copy-start
  2.0 1.7 copy-done
  3.7 0.0 copy-start.1
  3.7 1.6 copy-done.1
  5.3 0.0 copy-start.2
  5.3 0.7 copy-done.2
  6.0 269.4 %shard_map.77 = (bf16[2,2,32,16384]{3,2,1,0:T(8,128)(2,1)S(1)}, f32[160,32,128]{2,1,0:T(8,128)S(1)}) custom-call(bf16[2,2,256,1024]{3,2,1,0:T(8,128)(2,1)S(1)} %copy-done.1, bf16[2,2,32,16384]{3,2,1,0:T(8,128)(2,1)} %x_hbm.1, f32[160,32,128]{2,1,0:T(8,128)S(1)} %bitcast.6, f32[1280]{0:T(1024)S(1)} %copy-done.2, s32[2,128]{1,0:T(2,128)S(1)} %pad_add_fusion.gate), custom_call_target="tpu_custom_call" | custom-call | tf_op jit(solution)/shard_map/pallas_call | solution.py:249
  275.4 2.0 copy.10
  277.4 1.5 copy.11
Async XLA Ops:
  2.0 1.7 copy-start
  3.7 1.6 copy-start.1
  5.3 0.7 copy-start.2

commit v2 on v0

v2 whole, which is shorter than its diff:
```python
import functools

import numpy as np

import jax
import jax.numpy as jnp
from jax import lax
from jax.experimental import pallas as pl
from jax.experimental.pallas import tpu as pltpu
from jax.sharding import PartitionSpec as P

MESH = pl.DeviceIdType.MESH


def transform_tables(count, samples):
    sample_index = np.arange(samples)
    bin_index = samples // 4 + np.arange(count)
    phase = sample_index[None, :] * bin_index[:, None] % samples
    theta = 2.0 * np.pi / samples * phase
    scale = count ** (-0.5)
    return np.stack([scale * np.cos(theta), -scale * np.sin(theta)], 1).astype(np.float32)


def body(n, nf, factor, k_hbm, x_hbm, obs_hbm, table, gate, grad_hbm, mis,
         kbuf, xbuf, acc, pbuf, rbuf, fbuf, obuf, bsend, brecv, gbuf,
         lsem, ks, kr, xs, xr, ps, pr, bs, br, gs, gr):
    f = lax.axis_index("freq")
    me = lax.axis_index("vs")
    m = n // 2
    q = lax.rem(me, m)
    base = me - q
    partner = lax.rem(me + m, n)
    local_f, rw, span = kbuf.shape[1], kbuf.shape[3], kbuf.shape[4]
    samples, nv, half = obuf.shape

    k_copy = pltpu.make_async_copy(k_hbm, kbuf.at[0], lsem.at[0])
    o_copy = pltpu.make_async_copy(obs_hbm, obuf, lsem.at[1])

    def columns(j, b):
        block = lax.rem(j + b * m, n)
        return pl.ds(pl.multiple_of(block * span, span), span)

    def peer(d):
        return lax.rem(q + d, m)

    def origin(d):
        return lax.rem(q + m - d, m)

    def other(e):
        return lax.rem(f + e, nf)

    def receivers(h):
        return pl.ds(pl.multiple_of(h * half, half), half)

    def k_move(i, c):
        return pltpu.make_async_remote_copy(
            k_hbm.at[i, c], kbuf.at[1, i, c], ks.at[i, c], kr.at[i, c],
            device_id=(f, partner), device_id_type=MESH)

    def x_move(t, b, slot):
        return pltpu.make_async_remote_copy(
            x_hbm.at[:, :, :, columns(base + t, b)], xbuf.at[b, :, slot],
            xs.at[t, b], xr.at[slot, b],
            device_id=(f, base + t), device_id_type=MESH)

    def p_move(t, h, i, slot, lane):
        return pltpu.make_async_remote_copy(
            pbuf.at[t, h, i], rbuf.at[slot, lane, i], ps.at[t, h, i], pr.at[slot, lane, i],
            device_id=(h, base + t), device_id_type=MESH)

    def b_move(t, h, slot, lane):
        return pltpu.make_async_remote_copy(
            bsend.at[h], brecv.at[:, slot, :, :, receivers(lane)],
            bs.at[t, h], br.at[slot, lane],
            device_id=(h, base + t), device_id_type=MESH)

    def g_move(t, b, slot):
        return pltpu.make_async_remote_copy(
            gbuf.at[b, t], grad_hbm.at[:, :, :, columns(base + slot, b)],
            gs.at[t, b], gr.at[slot, b],
            device_id=(f, base + t), device_id_type=MESH)

    x_own = [pltpu.make_async_copy(
        x_hbm.at[:, :, :, columns(me, b)], xbuf.at[b, :, q], xr.at[q, b]) for b in range(2)]
    p_own = [pltpu.make_async_copy(
        pbuf.at[q, f, i], rbuf.at[q, f, i], pr.at[q, f, i]) for i in range(local_f)]
    b_own = pltpu.make_async_copy(
        bsend.at[f], brecv.at[:, q, :, :, receivers(f)], br.at[q, f])
    g_own = [pltpu.make_async_copy(
        gbuf.at[b, q], grad_hbm.at[:, :, :, columns(me, b)], gr.at[q, b]) for b in range(2)]

    barrier = pltpu.get_barrier_semaphore()
    pl.semaphore_signal(barrier, inc=1, device_id=(f, partner), device_id_type=MESH)
    for e in range(1, nf):
        pl.semaphore_signal(barrier, inc=1, device_id=(other(e), me), device_id_type=MESH)

    @pl.loop(1, m)
    def _(d):
        for e in range(nf):
            pl.semaphore_signal(
                barrier, inc=1, device_id=(other(e), base + peer(d)), device_id_type=MESH)

    k_copy.start()
    x_own[0].start()
    x_own[1].start()
    o_copy.start()
    pl.semaphore_wait(barrier, m * nf)

    pieces = [(i, c) for i in range(local_f) for c in range(2)]
    for step, (i, c) in enumerate(pieces):
        k_move(i, c).start()
        low = 1 + (m - 1) * step // len(pieces)
        high = 1 + (m - 1) * (step + 1) // len(pieces)

        @pl.loop(low, high)
        def _(d):
            for b in range(2):
                x_move(peer(d), b, q).start()

    k_copy.wait()
    for b in range(2):
        x_own[b].wait()

        @pl.loop(1, m)
        def _(d):
            x_move(origin(d), b, origin(d)).wait_recv()

    def product(b, i, c):
        rows = xbuf[b, i].reshape(m * 2 * nv, span)
        out = lax.dot_general(rows, kbuf[b, i, c], (((1,), (1,)), ((), ())),
                              preferred_element_type=jnp.float32)
        return out.reshape(m, 2, nv, rw)

    for i, c in pieces:
        acc[i, c] = product(0, i, c)

    for i in range(local_f):
        for c in range(2):
            k_move(i, c).wait_recv()
            acc[i, c] += product(1, i, c)

        @pl.loop(0, m)
        def _(t):
            real = (acc[i, 0, t, 0] - acc[i, 1, t, 1]).astype(jnp.bfloat16)
            imag = (acc[i, 0, t, 1] + acc[i, 1, t, 0]).astype(jnp.bfloat16)
            for h in range(nf):
                pbuf[t, h, i, 0] = real[:, h * half:(h + 1) * half]
                pbuf[t, h, i, 1] = imag[:, h * half:(h + 1) * half]

        @pl.loop(1, m)
        def _(d):
            for e in range(nf):
                p_move(peer(d), other(e), i, q, f).start()

        for e in range(1, nf):
            p_move(q, other(e), i, q, f).start()
        p_own[i].start()

    for i in range(local_f):
        p_own[i].wait()
        for e in range(1, nf):
            p_move(q, other(e), i, q, other(e)).wait_recv()

        @pl.loop(1, m)
        def _(d):
            for e in range(nf):
                p_move(origin(d), other(e), i, origin(d), other(e)).wait_recv()

    for h in range(nf):
        for i in range(local_f):
            for c in range(2):
                def add(t, total):
                    return total + rbuf[t, h, i, c].astype(jnp.float32)
                total = lax.fori_loop(0, m, add, jnp.zeros((nv, half), jnp.float32))
                fbuf[h * local_f + i, c] = total.astype(jnp.bfloat16).astype(jnp.float32)

    o_copy.wait()
    count = nf * local_f
    opens = gate[0:1, :]
    closes = gate[1:2, :]
    rows = 16
    for part in range(nv // rows):
        sl = slice(part * rows, (part + 1) * rows)
        fields = [fbuf[k, c, sl] for k in range(count) for c in range(2)]

        def sample(t, totals):
            weights = [table[k * samples + t] for k in range(2 * count)]
            signal = fields[0] * weights[0]
            for k in range(1, 2 * count):
                signal = signal + fields[k] * weights[k]
            inside = (opens <= t) & (t < closes)
            misfit = jnp.where(inside, signal - obuf[t, sl], 0.0)
            mis[t, sl] = misfit
            return tuple(totals[k] + misfit * weights[k] for k in range(2 * count))

        zero = jnp.zeros((rows, half), jnp.float32)
        totals = lax.fori_loop(0, samples, sample, (zero,) * (2 * count))
        for k in range(count):
            for c in range(2):
                bsend[k // local_f, k % local_f, c, sl] = totals[2 * k + c].astype(jnp.bfloat16)

    @pl.loop(1, m)
    def _(d):
        for e in range(nf):
            b_move(peer(d), other(e), q, f).start()

    b_own.start()
    for e in range(1, nf):
        b_move(q, other(e), q, f).start()

    def backward(t):
        for b in range(2):
            for i in range(local_f):
                left = brecv[i, t].reshape(2 * nv, rw)
                one = jnp.dot(left, kbuf[b, i, 0], preferred_element_type=jnp.float32)
                two = jnp.dot(left, kbuf[b, i, 1], preferred_element_type=jnp.float32)
                real = factor * (one[:nv] + two[nv:])
                imag = factor * (one[nv:] - two[:nv])
                gbuf[b, t, i, 0] = real.astype(jnp.bfloat16)
                gbuf[b, t, i, 1] = imag.astype(jnp.bfloat16)

    @pl.loop(1, m)
    def _(d):
        t = origin(d)
        for e in range(nf):
            b_move(t, other(e), t, other(e)).wait_recv()
        backward(t)
        for b in range(2):
            g_move(t, b, q).start()

    b_own.wait()
    for e in range(1, nf):
        b_move(q, other(e), q, other(e)).wait_recv()
    backward(q)
    for b in range(2):
        g_own[b].start()

    for i, c in pieces:
        k_move(i, c).wait_send()
    for e in range(1, nf):
        for i in range(local_f):
            p_move(q, other(e), i, q, f).wait_send()
        b_move(q, other(e), q, f).wait_send()

    @pl.loop(1, m)
    def _(d):
        t = origin(d)
        for e in range(nf):
            for i in range(local_f):
                p_move(t, other(e), i, q, f).wait_send()
            b_move(t, other(e), q, f).wait_send()
        for b in range(2):
            x_move(t, b, q).wait_send()
            g_move(t, b, q).wait_send()
            g_move(t, b, t).wait_recv()

    for b in range(2):
        g_own[b].wait()


def local(n, nf, kernel, sources, observed, gate_start, gate_length):
    local_f, _, rw, span = kernel.shape
    nv, ns = sources.shape[2:]
    half, samples = observed.shape[:2]
    count = nf * local_f
    m = n // 2
    table = jnp.asarray(transform_tables(count, samples).reshape(-1))
    gate = jnp.stack([gate_start, gate_start + gate_length])
    piece = (local_f, 2, nv, half)
    any_spec = pl.BlockSpec(memory_space=pl.ANY)
    hbm_spec = pl.BlockSpec(memory_space=pltpu.HBM)
    vmem_spec = pl.BlockSpec(memory_space=pltpu.VMEM)
    dma = pltpu.SemaphoreType.DMA
    gradient, misfit = pl.pallas_call(
        functools.partial(body, n, nf, (ns / rw) ** 0.5),
        out_shape=(
            jax.ShapeDtypeStruct(sources.shape, jnp.bfloat16),
            jax.ShapeDtypeStruct((samples, nv, half), jnp.float32),
        ),
        in_specs=[hbm_spec, hbm_spec, hbm_spec,
                  pl.BlockSpec(memory_space=pltpu.SMEM), vmem_spec],
        out_specs=(any_spec, vmem_spec),
        scratch_shapes=[
            pltpu.VMEM((2,) + kernel.shape, jnp.bfloat16),
            pltpu.VMEM((2, local_f, m, 2, nv, span), jnp.bfloat16),
            pltpu.VMEM((local_f, 2, m, 2, nv, rw), jnp.float32),
            pltpu.VMEM((m, nf) + piece, jnp.bfloat16),
            pltpu.VMEM((m, nf) + piece, jnp.bfloat16),
            pltpu.VMEM((count, 2, nv, half), jnp.float32),
            pltpu.VMEM((samples, nv, half), jnp.float32),
            pltpu.VMEM((nf,) + piece, jnp.bfloat16),
            pltpu.VMEM((local_f, m, 2, nv, nf * half), jnp.bfloat16),
            pltpu.VMEM((2, m, local_f, 2, nv, span), jnp.bfloat16),
            dma((2,)), dma((local_f, 2)), dma((local_f, 2)),
            dma((m, 2)), dma((m, 2)),
            dma((m, nf, local_f)), dma((m, nf, local_f)),
            dma((m, nf)), dma((m, nf)),
            dma((m, 2)), dma((m, 2)),
        ],
        compiler_params=pltpu.CompilerParams(
            collective_id=0, has_side_effects=True, vmem_limit_bytes=44 << 20),
    )(kernel, sources, observed.transpose(1, 2, 0), table, gate)
    return gradient, misfit.transpose(2, 0, 1)


def solution(mesh):
    n, nf = mesh.shape["vs"], mesh.shape["freq"]
    return jax.shard_map(
        functools.partial(local, n, nf),
        mesh=mesh,
        in_specs=(
            P("freq", None, None, "vs"),
            P("freq", None, "vs", None),
            P("freq", None, "vs"),
            P("freq"),
            P("freq"),
        ),
        out_specs=(P("freq", None, "vs", None), P("freq", None, "vs")),
        check_vma=False,
    )
```

time: 470 us -> 213 us (0.45)
  waiting for transfers between devices: 365 us -> 0 us
  Pallas kernels: 0 us -> 201 us
  matrix products: 72.3 us -> 0 us
  between operations: 14.2 us -> 0.64 us
  blocking collectives: 7.71 us -> 0 us
    all_gather x1 -> x0, waiting for transfers between devices: 365 us -> none  [local(): gathered = lax.all_gather(kernel, 'vs', axis=3, tiled=True)]
    pallas_call x0 -> x1, Pallas kernels: none -> 201 us  [local(): pl.pallas_call(functools.partial(body, n, nf, (ns / rw) ** 0.5), out_shap...]
    dot_general x12 -> x0, matrix products: 72.3 us -> none  [the longest x1 9.96 us: complex_apply(): jnp.einsum(form, kern[:, 0], model[:, 1], preferred_element_type=jnp.floa...]
    all_to_all x2 -> x0, blocking collectives: 7.71 us -> none  [the longest x1 3.92 us: local(): lax.all_to_all(field, 'freq', split_axis=2, concat_axis=0, tiled=True)]
    unnamed x13 -> x8, local copies, waits for them, and re-layouts: 8.92 us -> 10.1 us
  transfers between devices with their start and end apart: 1 -> 0, of which waited for: 1 -> 0; matrix products, arithmetic and copies ran while one was open for 0% -> 0% of each run, Pallas kernels for 0% -> 0%
where the time goes in v2:
time: 213 us
  Pallas kernels  201 us (94%)
  local copies, waits for them, and re-layouts  10.1 us (5%)
    pallas_call x1, Pallas kernels, local(): pl.pallas_call(functools.partial(body, n, nf, (ns / rw) ** 0.5), out_shap...  201 us
    unnamed x8, local copies, waits for them, and re-layouts  10.1 us

profile of v2, /device:TPU:0, one launch (start us, length us, event | category | flops | bytes accessed | tf_op | source)
XLA Modules:
  0.0 213.1 jit_solution(16231751314550937075)
XLA Ops:
  0.6 0.7 add_bitcast_fusion
  1.3 0.7 pad_add_fusion.gate
  2.0 0.0 copy-start
  2.0 1.7 copy-done
  3.7 0.0 copy-start.1
  3.7 1.6 copy-done.1
  5.3 0.0 copy-start.2
  5.3 0.7 copy-done.2
  6.0 201.0 %shard_map.77 = (bf16[2,2,32,16384]{3,2,1,0:T(8,128)(2,1)}, f32[160,32,128]{2,1,0:T(8,128)S(1)}) custom-call(bf16[2,2,256,1024]{3,2,1,0:T(8,128)(2,1)S(1)} %copy-done.1, bf16[2,2,32,16384]{3,2,1,0:T(8,128)(2,1)} %x_hbm.1, f32[160,32,128]{2,1,0:T(8,128)S(1)} %bitcast.6, f32[1280]{0:T(1024)S(1)} %copy-done.2, s32[2,128]{1,0:T(2,128)S(1)} %pad_add_fusion.gate), custom_call_target="tpu_custom_call" | custom-call | tf_op jit(solution)/shard_map/pallas_call | solution.py:274
  207.1 4.6 %copy.10 = bf16[2,2,32,16384]{3,2,1,0:T(8,128)(2,1)} copy(bf16[2,2,32,16384]{3,2,1,0:T(8,128)(2,1)} %get-tuple-element.8) | data formatting | bytes 8388608
  211.6 1.5 copy.11
Async XLA Ops:
  2.0 1.7 copy-start
  3.7 1.6 copy-start.1
  5.3 0.7 copy-start.2

commit v3 on v2

--- a/solution.py
+++ b/solution.py
@@ -21,9 +21,9 @@
     return np.stack([scale * np.cos(theta), -scale * np.sin(theta)], 1).astype(np.float32)
 
 
-def body(n, nf, factor, k_hbm, x_hbm, obs_hbm, table, gate, grad_hbm, mis,
+def body(n, nf, factor, k_hbm, x_hbm, obs_hbm, table_hbm, start_hbm, length_hbm, grad_hbm, mis,
          kbuf, xbuf, acc, pbuf, rbuf, fbuf, obuf, bsend, brecv, gbuf,
-         lsem, ks, kr, xs, xr, ps, pr, bs, br, gs, gr):
+         table, gate, lsem, ks, kr, xs, xr, ps, pr, bs, br, gs, gr):
     f = lax.axis_index("freq")
     me = lax.axis_index("vs")
     m = n // 2
@@ -35,16 +35,34 @@
 
     k_copy = pltpu.make_async_copy(k_hbm, kbuf.at[0], lsem.at[0])
     o_copy = pltpu.make_async_copy(obs_hbm, obuf, lsem.at[1])
+    small = [
+        pltpu.make_async_copy(table_hbm, table, lsem.at[2]),
+        pltpu.make_async_copy(start_hbm, gate.at[0], lsem.at[3]),
+        pltpu.make_async_copy(length_hbm, gate.at[1], lsem.at[4]),
+    ]
 
     def columns(j, b):
         block = lax.rem(j + b * m, n)
         return pl.ds(pl.multiple_of(block * span, span), span)
 
-    def peer(d):
-        return lax.rem(q + d, m)
-
-    def origin(d):
-        return lax.rem(q + m - d, m)
+    def peer(s):
+        s = jnp.int32(s) - 1
+        odd = lax.rem(s, 2)
+        low = lax.div(s, 2)
+        d = odd * (low + 1) + (1 - odd) * (m - 1 - low)
+        if m & (m - 1):
+            return lax.rem(q + d, m)
+        t = jnp.int32(0)
+        bit = 1
+        while bit < m:
+            t = t + bit * lax.rem(lax.div(q, bit) + lax.div(d, bit), 2)
+            bit *= 2
+        return t
+
+    def origin(s):
+        if m & (m - 1):
+            return lax.rem(2 * q + m - peer(s), m)
+        return peer(s)
 
     def other(e):
         return lax.rem(f + e, nf)
@@ -53,8 +71,10 @@
         return pl.ds(pl.multiple_of(h * half, half), half)
 
     def k_move(i, c):
-        return pltpu.make_async_remote_copy(
-            k_hbm.at[i, c], kbuf.at[1, i, c], ks.at[i, c], kr.at[i, c],
+        g, c = c // 2, c % 2
+        rows = pl.ds(g * (rw // 2), rw // 2)
+        return pltpu.make_async_remote_copy(
+            k_hbm.at[i, c, rows], kbuf.at[1, i, c, rows], ks.at[i, c, g], kr.at[i, c, g],
             device_id=(f, partner), device_id_type=MESH)
 
     def x_move(t, b, slot):
@@ -104,11 +124,16 @@
     x_own[0].start()
     x_own[1].start()
     o_copy.start()
+    for copy in small:
+        copy.start()
     pl.semaphore_wait(barrier, m * nf)
 
-    pieces = [(i, c) for i in range(local_f) for c in range(2)]
+    pieces = [(i, c) for i in range(local_f) for c in range(4)]
+    k_move(*pieces[0]).start()
+    k_move(*pieces[1]).start()
     for step, (i, c) in enumerate(pieces):
-        k_move(i, c).start()
+        if step >= 2:
+            k_move(i, c).start()
         low = 1 + (m - 1) * step // len(pieces)
         high = 1 + (m - 1) * (step + 1) // len(pieces)
 
@@ -131,12 +156,14 @@
                               preferred_element_type=jnp.float32)
         return out.reshape(m, 2, nv, rw)
 
-    for i, c in pieces:
-        acc[i, c] = product(0, i, c)
+    for i in range(local_f):
+        for c in range(2):
+            acc[i, c] = product(0, i, c)
 
     for i in range(local_f):
         for c in range(2):
             k_move(i, c).wait_recv()
+            k_move(i, c + 2).wait_recv()
             acc[i, c] += product(1, i, c)
 
         @pl.loop(0, m)
@@ -175,9 +202,11 @@
                 fbuf[h * local_f + i, c] = total.astype(jnp.bfloat16).astype(jnp.float32)
 
     o_copy.wait()
+    for copy in small:
+        copy.wait()
     count = nf * local_f
-    opens = gate[0:1, :]
-    closes = gate[1:2, :]
+    opens = gate[0]
+    closes = opens + gate[1]
     rows = 16
     for part in range(nv // rows):
         sl = slice(part * rows, (part + 1) * rows)
@@ -194,7 +223,7 @@
             return tuple(totals[k] + misfit * weights[k] for k in range(2 * count))
 
         zero = jnp.zeros((rows, half), jnp.float32)
-        totals = lax.fori_loop(0, samples, sample, (zero,) * (2 * count))
+        totals = lax.fori_loop(0, samples, sample, (zero,) * (2 * count), unroll=4)
         for k in range(count):
             for c in range(2):
                 bsend[k // local_f, k % local_f, c, sl] = totals[2 * k + c].astype(jnp.bfloat16)
@@ -265,9 +294,10 @@
     count = nf * local_f
     m = n // 2
     table = jnp.asarray(transform_tables(count, samples).reshape(-1))
-    gate = jnp.stack([gate_start, gate_start + gate_length])
+    gate_shape = (1, half)
+    mis_shape = (samples, nv, half)
+    held = 2 * sources.size + 4 * observed.size
     piece = (local_f, 2, nv, half)
-    any_spec = pl.BlockSpec(memory_space=pl.ANY)
     hbm_spec = pl.BlockSpec(memory_space=pltpu.HBM)
     vmem_spec = pl.BlockSpec(memory_space=pltpu.VMEM)
     dma = pltpu.SemaphoreType.DMA
@@ -275,11 +305,11 @@
         functools.partial(body, n, nf, (ns / rw) ** 0.5),
         out_shape=(
             jax.ShapeDtypeStruct(sources.shape, jnp.bfloat16),
-            jax.ShapeDtypeStruct((samples, nv, half), jnp.float32),
+            jax.ShapeDtypeStruct(mis_shape, jnp.float32),
         ),
         in_specs=[hbm_spec, hbm_spec, hbm_spec,
-                  pl.BlockSpec(memory_space=pltpu.SMEM), vmem_spec],
-        out_specs=(any_spec, vmem_spec),
+                  hbm_spec, hbm_spec, hbm_spec],
+        out_specs=(vmem_spec, vmem_spec),
         scratch_shapes=[
             pltpu.VMEM((2,) + kernel.shape, jnp.bfloat16),
             pltpu.VMEM((2, local_f, m, 2, nv, span), jnp.bfloat16),
@@ -291,15 +321,18 @@
             pltpu.VMEM((nf,) + piece, jnp.bfloat16),
             pltpu.VMEM((local_f, m, 2, nv, nf * half), jnp.bfloat16),
             pltpu.VMEM((2, m, local_f, 2, nv, span), jnp.bfloat16),
-            dma((2,)), dma((local_f, 2)), dma((local_f, 2)),
+            pltpu.SMEM((2 * count * samples,), jnp.float32),
+            pltpu.VMEM((2,) + gate_shape, jnp.int32),
+            dma((5,)), dma((local_f, 2, 2)), dma((local_f, 2, 2)),
             dma((m, 2)), dma((m, 2)),
             dma((m, nf, local_f)), dma((m, nf, local_f)),
             dma((m, nf)), dma((m, nf)),
             dma((m, 2)), dma((m, 2)),
         ],
         compiler_params=pltpu.CompilerParams(
-            collective_id=0, has_side_effects=True, vmem_limit_bytes=44 << 20),
-    )(kernel, sources, observed.transpose(1, 2, 0), table, gate)
+            collective_id=0, has_side_effects=True, vmem_limit_bytes=67043328 - held - (1 << 20)),
+    )(kernel, sources, observed.transpose(1, 2, 0), table,
+      gate_start.reshape(gate_shape), gate_length.reshape(gate_shape))
     return gradient, misfit.transpose(2, 0, 1)
 
 

time: 213 us -> 181 us (0.85)
  Pallas kernels: 201 us -> 174 us
  local copies, waits for them, and re-layouts: 10.1 us -> 6.22 us
    pallas_call x1, Pallas kernels: 201 us -> 174 us  [local(): pl.pallas_call(functools.partial(body, n, nf, (ns / rw) ** 0.5), out_shap...]
    unnamed x8 -> x4, local copies, waits for them, and re-layouts: 10.1 us -> 6.22 us
where the time goes in v3:
time: 181 us
  Pallas kernels  174 us (96%)
  local copies, waits for them, and re-layouts  6.22 us (3%)
    pallas_call x1, Pallas kernels, local(): pl.pallas_call(functools.partial(body, n, nf, (ns / rw) ** 0.5), out_shap...  174 us
    unnamed x4, local copies, waits for them, and re-layouts  6.22 us

profile of v3, /device:TPU:0, one launch (start us, length us, event | category | flops | bytes accessed | tf_op | source)
XLA Modules:
  0.0 180.9 jit_solution(1151062643330425295)
XLA Ops:
  0.6 174.1 %shard_map.77 = (bf16[2,2,32,16384]{3,2,1,0:T(8,128)(2,1)}, f32[160,32,128]{2,1,0:T(8,128)}) custom-call(bf16[2,2,256,1024]{3,2,1,0:T(8,128)(2,1)} %k_hbm.1, bf16[2,2,32,16384]{3,2,1,0:T(8,128)(2,1)} %x_hbm.1, f32[160,32,128]{2,1,0:T(8,128)} %bitcast.5, f32[1280]{0:T(1024)} %constant.2.clone.table_hbm, s32[1,128]{1,0:T(1,128)} %bitcast.6, s32[1,128]{1,0:T(1,128)} %bitcast.7), custom_call_target="tpu_custom_call" | custom-call | tf_op jit(solution)/shard_map/pallas_call | solution.py:304
  174.7 0.0 copy-start
  174.7 4.7 %copy.10 = bf16[2,2,32,16384]{3,2,1,0:T(8,128)(2,1)} copy(bf16[2,2,32,16384]{3,2,1,0:T(8,128)(2,1)} %get-tuple-element.8) | data formatting | bytes 8388608
  179.5 0.0 copy-done
  179.5 1.5 copy.11
Async XLA Ops:
  174.7 4.7 %copy-start = (f32[160,32,128]{2,1,0:T(8,128)S(1)}, f32[160,32,128]{2,1,0:T(8,128)}, u32[]{:S(2)}) copy-start(f32[160,32,128]{2,1,0:T(8,128)} %get-tuple-element.5) | copy-start | bytes 7864324
